TPU v7x, 256 devices: a whole 4x4x8 slice. The times are simulated.
256 devices in a mesh: dp: 64 (over z, y, core), mp: 4 (over x).
Axes of the slice: x: 4, y: 4, z: 8, core: 2. Of those that a mesh axis runs over, the one named last changes fastest.
Arguments:
- noise_blocks: bfloat16 [512, 12800], P('dp'), may hold values from -6 to 6
- data_blocks: bfloat16 [512, 12800], P('dp'), may hold values from -6 to 6
- destination: int32 [512], replicated, may hold values from 0 to 511, as said below
- utt_blocks: int32 [64, 4], P('dp'), may hold values from 1 to 4, 8 in all within a row
- span_start: int32 [64, 4], P('dp'), may hold values from 0 to 19
- span_size: int32 [64, 4], P('dp'), may hold values from 44 to 64
- timestep: int32 [64, 4], P('dp'), may hold values from 1 to 63
- in_weight: bfloat16 [200, 1024], replicated, may hold values from -0.4375 to 0.4375
- norm_gain: bfloat16 [1024], replicated, may hold values from 0.5 to 1.5
- qkv_weight: bfloat16 [1024, 3, 512], P(None, None, 'mp'), may hold values from -4 to 4
- out_proj: bfloat16 [512, 1024], P('mp'), may hold values from -0.25 to 0.25
- final_gain: bfloat16 [1024], replicated, may hold values from 0.25 to 1.75
- vel_weight: bfloat16 [1024, 100], replicated, may hold values from -0.1875 to 0.1875
Outputs:
- grad_qkv: float32 [1024, 3, 512], P('dp', None, 'mp')
- grad_out: float32 [512, 1024], P('mp', 'dp')
Inputs may be any that keep to these rules, and one draw needn't show every extreme that they name: `destination`: A permutation of the 512 bin positions; a device sends to each bin either none or exactly 1 of its blocks.
All inputs are finite; a program needn't handle non-finite values.
Results may differ from a plain program's by a relative error of at most 0.004.
Values may be sent and summed in bfloat16 or wider, within the bound.
No kernel may reach another device: no remote copies, remote signals or barrier semaphores. Data moves between devices by JAX's collectives and lax.ppermute only.
A program may use at most 64 MiB of HBM per device.

v0:
```python
import jax
import jax.numpy as jnp
from jax import lax
from jax.sharding import PartitionSpec as P

HEAD_DIM = 64
BLOCK = 128


def sent_together(arrays, axis, split_dim, concat_dim, along):
    widths = [a.shape[along] for a in arrays]
    both = jnp.concatenate(arrays, axis=along)
    out = lax.all_to_all(both, axis, split_axis=split_dim, concat_axis=concat_dim, tiled=True)
    return tuple(jnp.split(out, [sum(widths[:k]) for k in range(1, len(widths))], axis=along))


def sent_together_2(arrays, axis, dim, along):
    both = jnp.concatenate(arrays, axis=along)
    out, at, finished = (lax.all_gather(both, axis, axis=dim, tiled=True), 0, [])
    for a in arrays:
        finished.append(lax.slice_in_dim(out, at, at + a.shape[along], axis=along))
        at += a.shape[along]
    return tuple(finished)


def sent_to_all(shard, axis):
    length = lax.axis_size(axis)
    return lax.all_to_all(
        jnp.broadcast_to(shard[None], (length, *shard.shape)), axis, 0, 0, tiled=True
    )


def of_everyone(shard, axis):
    return sent_to_all(shard, axis).sum(axis=0)


def split_up(shard, dim, length):
    dims = shard.shape
    tiles = shard.reshape(*dims[:dim], length, dims[dim] // length, *dims[dim + 1 :])
    return jnp.moveaxis(tiles, dim, 0)


def sent_and_summed(shard, axis, dim):
    length = lax.axis_size(axis)
    tiles = lax.all_to_all(split_up(shard, dim, length), axis, 0, 0, tiled=True)
    return jnp.sum(tiles, axis=0)


def frame_table(lengths, starts, sizes, steps, rows):
    ends = jnp.cumsum(lengths)
    frame = jnp.arange(rows, dtype=jnp.int32)
    block_index = frame // BLOCK
    segment = jnp.sum((block_index[:, None] >= ends[None, :]).astype(jnp.int32), axis=1)
    member = segment[:, None] == jnp.arange(lengths.shape[0], dtype=jnp.int32)[None, :]
    first = jnp.sum(jnp.where(member, (ends - lengths)[None, :], 0), axis=1) * BLOCK
    span = jnp.sum(jnp.where(member, lengths[None, :], 0), axis=1) * BLOCK
    lower = jnp.sum(jnp.where(member, starts[None, :], 0), axis=1)
    upper = lower + jnp.sum(jnp.where(member, sizes[None, :], 0), axis=1)
    inside = 64 * (frame - first)
    masked = ((inside >= lower * span) & (inside < upper * span)).astype(jnp.float32)
    level = jnp.sum(jnp.where(member, steps[None, :], 0), axis=1).astype(jnp.float32) / 64.0
    return (segment, masked, level)


def attend(query, keys, values, segment):
    rows, width = query.shape
    heads = width // HEAD_DIM
    block = min(512, rows)
    reach = min(4, rows // BLOCK // 2) * BLOCK
    window = min(rows, block + 2 * reach)
    blocks = rows // block
    query_blocks = query.reshape(blocks, block, heads, HEAD_DIM)
    segment_blocks = segment.reshape(blocks, block)
    firsts = jnp.clip(jnp.arange(blocks, dtype=jnp.int32) * block - reach, 0, rows - window)
    keyed = keys.reshape(rows, heads, HEAD_DIM)
    valued = values.reshape(rows, heads, HEAD_DIM)

    def one_block(item):
        query_block, segment_block, first = item
        scores = jnp.einsum(
            "qhd,khd->hqk", query_block, keyed, preferred_element_type=jnp.float32
        ) * HEAD_DIM ** (-0.5)
        scores = jnp.where((segment_block[:, None] == segment[None, :])[None], scores, -1e30)
        top = jnp.max(scores, axis=-1, keepdims=True)
        weights = jnp.exp(scores - top)
        probs = (weights / jnp.sum(weights, axis=-1, keepdims=True)).astype(jnp.bfloat16)
        return jnp.einsum(
            "hqk,khd->qhd", probs, valued, preferred_element_type=jnp.float32
        ).reshape(block, width)

    return lax.map(jax.checkpoint(one_block), (query_blocks, segment_blocks, firsts)).reshape(
        rows, width
    )


def shards(
    noise_blocks,
    data_blocks,
    destination,
    utt_blocks,
    span_start,
    span_size,
    timestep,
    in_weight,
    norm_gain,
    qkv_weight,
    out_proj,
    final_gain,
    vel_weight,
):
    sources = lax.axis_size("dp")
    here = lax.axis_index("dp")
    per_dev = noise_blocks.shape[0]
    depth = max(1, per_dev // sources)
    lanes_total = sources * depth
    table = destination.reshape(sources, per_dev)
    owner = table // per_dev
    order = jnp.arange(per_dev, dtype=jnp.int32)
    earlier = (owner[:, :, None] == owner[:, None, :]) & (
        order[None, None, :] < order[None, :, None]
    )
    rank = jnp.sum(earlier.astype(jnp.int32), axis=2)
    code = jnp.arange(sources, dtype=jnp.int32)[:, None] * depth + rank
    mine_owner = lax.dynamic_index_in_dim(owner, here, 0, keepdims=False)
    mine_rank = lax.dynamic_index_in_dim(rank, here, 0, keepdims=False)
    lanes = jnp.arange(lanes_total, dtype=jnp.int32)
    packing = (lanes[:, None] == (mine_owner * depth + mine_rank)[None, :]).astype(jnp.bfloat16)
    wanted = here * per_dev + order
    hit = table[None, :, :] == wanted[:, None, None]
    source_code = jnp.sum(jnp.where(hit, code[None, :, :], 0), axis=(1, 2))
    unpacking = (source_code[:, None] == lanes[None, :]).astype(jnp.bfloat16)

    def outgoing(blocks):
        sent = jnp.dot(packing, blocks, preferred_element_type=jnp.float32).astype(jnp.bfloat16)
        return sent.reshape(sources, depth, blocks.shape[1])

    def incoming(arrived):
        flat = arrived.reshape(lanes_total, arrived.shape[2])
        return jnp.dot(unpacking, flat, preferred_element_type=jnp.float32).astype(jnp.bfloat16)

    share = noise_blocks.shape[1] // lax.axis_size("mp")
    offset = lax.axis_index("mp") * share
    noise_share = lax.dynamic_slice_in_dim(noise_blocks, offset, share, 1)
    data_share = lax.dynamic_slice_in_dim(data_blocks, offset, share, 1)
    got_noise, got_data = sent_together(
        (outgoing(noise_share), outgoing(data_share)), "dp", 0, 0, 1
    )
    bin_noise, bin_data = sent_together_2((incoming(got_noise), incoming(got_data)), "mp", 1, 0)
    rows = per_dev * BLOCK
    mel = noise_blocks.shape[1] // BLOCK
    noise = bin_noise.reshape(rows, mel).astype(jnp.float32)
    data = bin_data.reshape(rows, mel).astype(jnp.float32)
    segment, masked, level = frame_table(
        utt_blocks[0], span_start[0], span_size[0], timestep[0], rows
    )
    noisy = (1.0 - level[:, None]) * noise + level[:, None] * data
    cond = data * (1.0 - masked[:, None])
    target = data - noise
    inputs = jnp.concatenate([noisy, cond], axis=1).astype(jnp.bfloat16)
    hidden0 = jnp.dot(inputs, in_weight, preferred_element_type=jnp.float32)
    scale = lax.rsqrt(jnp.mean(hidden0 * hidden0, axis=1, keepdims=True) + 1e-06)
    normed = (hidden0 * scale * norm_gain.astype(jnp.float32)[None, :]).astype(jnp.bfloat16)
    query = jnp.dot(normed, qkv_weight[:, 0, :], preferred_element_type=jnp.float32).astype(
        jnp.bfloat16
    )
    keys = jnp.dot(normed, qkv_weight[:, 1, :], preferred_element_type=jnp.float32).astype(
        jnp.bfloat16
    )
    values = jnp.dot(normed, qkv_weight[:, 2, :], preferred_element_type=jnp.float32).astype(
        jnp.bfloat16
    )
    heads_out, pullback = jax.vjp(lambda a, b, c: attend(a, b, c, segment), query, keys, values)
    attended = heads_out.astype(jnp.bfloat16)
    partial_mix = jnp.dot(attended, out_proj, preferred_element_type=jnp.float32)
    mixed = lax.psum(partial_mix.astype(jnp.bfloat16), "mp").astype(jnp.float32)
    hidden1 = (hidden0 + mixed).astype(jnp.bfloat16)
    wide1 = lax.optimization_barrier(hidden1).astype(jnp.float32)
    rscale = lax.rsqrt(jnp.mean(wide1 * wide1, axis=1, keepdims=True) + 1e-06)
    normalized = wide1 * rscale
    gain_out = final_gain.astype(jnp.float32)[None, :]
    final = (normalized * gain_out).astype(jnp.bfloat16)
    velocity = jnp.dot(final, vel_weight, preferred_element_type=jnp.float32)
    count = of_everyone(jnp.sum(masked), "dp")
    error = (2.0 * masked[:, None] * (velocity - target)).astype(jnp.bfloat16)
    grad_final = jnp.dot(error, vel_weight.T, preferred_element_type=jnp.float32)
    scaled = grad_final * gain_out
    back1 = (
        rscale * (scaled - normalized * jnp.mean(scaled * normalized, axis=1, keepdims=True))
    ).astype(jnp.bfloat16)
    back_att = jnp.dot(back1, out_proj.T, preferred_element_type=jnp.float32).astype(jnp.bfloat16)
    dquery, dkeys, dvalues = pullback(back_att.astype(jnp.float32))
    out_terms = jnp.dot(attended.T, back1, preferred_element_type=jnp.float32)
    qkv_terms = jnp.stack(
        [
            jnp.dot(normed.T, dquery, preferred_element_type=jnp.float32),
            jnp.dot(normed.T, dkeys, preferred_element_type=jnp.float32),
            jnp.dot(normed.T, dvalues, preferred_element_type=jnp.float32),
        ],
        axis=1,
    )
    summed_qkv, summed_out = (
        sent_and_summed(qkv_terms, "dp", 0),
        sent_and_summed(out_terms, "dp", 1),
    )
    return (summed_qkv / count, summed_out / count)


def solution(mesh):
    in_specs = (
        P("dp", None),
        P("dp", None),
        P(),
        P("dp", None),
        P("dp", None),
        P("dp", None),
        P("dp", None),
        P(),
        P(),
        P(None, None, "mp"),
        P("mp", None),
        P(),
        P(),
    )
    out_specs = (P("dp", None, "mp"), P("mp", "dp"))
    return jax.shard_map(shards, mesh=mesh, in_specs=in_specs, out_specs=out_specs, check_vma=False)
```

profile of v0, /device:TPU:1, one launch (start us, length us, event | category | flops | bytes accessed | tf_op | source)
XLA Modules:
  0.0 277.2 jit_solution(8119586240358613834)
XLA Ops:
  7.3 0.8 eq.126
  8.4 1.1 fusion.62
  9.5 1.1 fusion.61
  10.7 1.7 copy.118
  12.4 13.2 %all-to-all-start = ((bf16[64,2,3200]{2,1,0:T(2,128)(2,1)}), bf16[64,2,3200]{2,1,0:T(2,128)(2,1)S(1)}, u32[]{:S(2)}, u32[]{:S(2)}) async-start(bf16[64,2,3200]{2,1,0:T(2,128)(2,1)} %copy.118), calls=%async_computation | async-start | bytes 1638400 | tf_op jit(solution)/shard_map/all_to_all | solution.py:13
  27.7 21.2 %all-to-all-done = bf16[64,2,3200]{2,1,0:T(2,128)(2,1)S(1)} async-done(((bf16[64,2,3200]{2,1,0:T(2,128)(2,1)}), bf16[64,2,3200]{2,1,0:T(2,128)(2,1)S(1)}, u32[]{:S(2)}, u32[]{:S(2)}) %all-to-all-start) | async-done | bytes 819232 | tf_op jit(solution)/shard_map/all_to_all | solution.py:13
  48.9 1.1 fusion.127
  50.5 11.4 %all_gather.3 = bf16[16,12800]{1,0:T(8,128)(2,1)S(1)} all-gather(bf16[16,3200]{1,0:T(8,128)(2,1)S(1)} %pad_maximum_fusion.2), channel_id=1, replica_groups=mesh['dp'=64,'mp'=4] {'mp'}, dimensions={1}, use_global_device_ids=true | all-gather | bytes 512000 | tf_op jit(solution)/shard_map/all_gather | solution.py:19
  61.9 0.9 reshape.364
  62.9 0.9 reshape.365
  64.3 0.9 multiply_reduce_fusion
  65.7 1.3 copy-done.27
  68.3 0.8 convolution_convert_fusion.9
  69.3 1.0 copy.127
  70.4 16.2 %while.30 = (s32[]{:T(128)}, bf16[2,512,128]{2,1,0:T(8,128)(2,1)S(1)}, s32[2,512]{1,0:T(2,128)S(1)}, s32[1,1024]{1,0:T(1,128)S(1)}, bf16[2,512,2,64]{1,3,2,0:T(8...) while((s32[]{:T(128)}, ...), condition=%wide.region_13.14_spmd, body=%wide.region_10.13_spmd.sunk | while | flops 275252224 | bytes 10766441 | solution.py:91
  70.7 4.5 %fusion.178 = (f32[2,512]{1,0:T(2,128)S(1)}, f32[2,512,1024]{2,1,0:T(8,128)}) fusion(pred[512,1024]{1,0:T(8,128)(4,1)S(1)} %broadcast_compare_fusion.4, bf16[1024,2,64]{0,2,1:T(8,128)(2,1)S(1)} %get-tuple-element.655, bf16[2,512,2,64]{1,3,2,0:T(8,128)(2,1)} %get-tuple-element.654, s32[]{:T(128)S(6)} %copy.175), kind=kOutput, calls=%fused_computation.183.clone.1 | convolution fusion | flops 138413056 | bytes 5115908 | tf_op jit(solution)/shard_map/jvp()/while/body/eval_jaxpr/sub | solution.py:85
  75.2 3.0 %fusion.179 = bf16[2,512,64]{1,2,0:T(8,128)(2,1)S(1)} fusion(bf16[1024,2,64]{0,2,1:T(8,128)(2,1)S(1)} %get-tuple-element.656, f32[2,512,1024]{2,1,0:T(8,128)} %get-tuple-element.608, f32[2,512]{1,0:T(2,128)S(1)} %get-tuple-element.609), kind=kOutput, calls=%fused_computation.8.clone.1 | convolution fusion | flops 136314880 | bytes 4591616 | tf_op jit(solution)/shard_map/jvp()/while/body/eval_jaxpr/hqk,khd->qhd/dot_general | solution.py:87
  78.8 4.5 %fusion.178 = (f32[2,512]{1,0:T(2,128)S(1)}, f32[2,512,1024]{2,1,0:T(8,128)}) fusion(pred[512,1024]{1,0:T(8,128)(4,1)S(1)} %broadcast_compare_fusion.4, bf16[1024,2,64]{0,2,1:T(8,128)(2,1)S(1)} %get-tuple-element.655, bf16[2,512,2,64]{1,3,2,0:T(8,128)(2,1)} %get-tuple-element.654, s32[]{:T(128)S(6)} %copy.175), kind=kOutput, calls=%fused_computation.183.clone.1 | convolution fusion | flops 138413056 | bytes 5115908 | tf_op jit(solution)/shard_map/jvp()/while/body/eval_jaxpr/sub | solution.py:85
  83.3 3.0 %fusion.179 = bf16[2,512,64]{1,2,0:T(8,128)(2,1)S(1)} fusion(bf16[1024,2,64]{0,2,1:T(8,128)(2,1)S(1)} %get-tuple-element.656, f32[2,512,1024]{2,1,0:T(8,128)} %get-tuple-element.608, f32[2,512]{1,0:T(2,128)S(1)} %get-tuple-element.609), kind=kOutput, calls=%fused_computation.8.clone.1 | convolution fusion | flops 136314880 | bytes 4591616 | tf_op jit(solution)/shard_map/jvp()/while/body/eval_jaxpr/hqk,khd->qhd/dot_general | solution.py:87
  86.6 2.1 convolution_convert_fusion.5
  88.7 1.3 broadcast_in_dim.203
  90.0 8.7 %all-to-all-start.2 = ((f32[64,1,1]{2,1,0:T(1,128)}), f32[64,1,1]{2,1,0:T(1,128)}, u32[]{:S(2)}, u32[]{:S(2)}) async-start(f32[64,1,1]{2,1,0:T(1,128)} %broadcast_in_dim.203), calls=%async_computation.2 | async-start | bytes 65536 | tf_op jit(solution)/shard_map/all_to_all | solution.py:28
  99.3 1.0 copy.126
  100.3 1.0 copy.125
  101.4 49.6 %all-reduce.2.cloned.1.call-done = bf16[1024,1024]{0,1:T(8,128)(2,1)} async-done(((bf16[1024,1024]{0,1:T(8,128)(2,1)}), bf16[1024,1024]{0,1:T(8,128)(2,1)}) %all-reduce.2.cloned.1.call-update) | async-done | bytes 2097168 | tf_op jit(solution)/shard_map/psum | solution.py:175
  151.0 3.6 %add_convert_fusion = bf16[1024,1024]{0,1:T(8,128)(2,1)S(1)} fusion(f32[1024,1024]{0,1:T(8,128)} %copy-done.1, bf16[1024,1024]{0,1:T(8,128)(2,1)} %all-reduce.2.cloned.1.call-done), kind=kLoop, calls=%fused_computation.86 | loop fusion | flops 3145728 | bytes 8388608 | tf_op jit(solution)/shard_map/convert_element_type | solution.py:176
  155.1 4.4 %fusion.64 = (f32[1024]{0:T(1024)S(1)}, f32[1024,1024]{0,1:T(8,128)}) fusion(bf16[1024,1024]{0,1:T(8,128)(2,1)S(1)} %add_convert_fusion, f32[1024]{0:T(1024)S(1)} %copy-done.19, f32[1024]{0:T(1024)S(1)} %add_rsqrt_fusion, bf16[1024,100]{0,1:T(8,128)(2,1)} %param.29, f32[1024,100]{0,1:T(8,128)S(1)} %copy-done.10, f32[1024,100]{0,1:T(8,128)S(1)} %copy-done.9, ...), kind=kOutput, calls=%fused_computation.81 | convolution fusion | flops 429276160 | bytes 7331840 | tf_op jit(solution)/shard_map/dot_general | solution.py:185
  159.5 3.2 %fusion.67 = bf16[1024,1024]{0,1:T(8,128)(2,1)S(1)} fusion(bf16[1024,1024]{0,1:T(8,128)(2,1)S(1)} %add_convert_fusion, f32[1024,1024]{0,1:T(8,128)} %get-tuple-element.497, f32[1024]{0:T(1024)S(1)} %broadcast_multiply_fusion, f32[1024]{0:T(1024)S(1)} %copy-done.19, f32[1024]{0:T(1024)S(1)} %add_rsqrt_fusion), kind=kLoop, calls=%fused_computation.84 | loop fusion | flops 7340032 | bytes 8400896 | tf_op jit(solution)/shard_map/convert_element_type | solution.py:189
  162.7 2.3 fusion.75
  165.0 0.8 convolution_convert_fusion.6
  165.8 1.1 copy.136
  166.9 10.9 %all-to-all-start.3 = ((f32[64,128,16]{1,2,0:T(8,128)}), f32[64,128,16]{1,2,0:T(8,128)}, u32[]{:S(2)}, u32[]{:S(2)}) async-start(f32[64,128,16]{1,2,0:T(8,128)} %copy.136), calls=%async_computation.3 | async-start | bytes 1048576 | tf_op jit(solution)/shard_map/all_to_all | solution.py:45
  178.5 33.6 %while.31 = (s32[]{:T(128)}, bf16[1024,2,64]{0,2,1:T(8,128)(2,1)}, bf16[1024,2,64]{0,2,1:T(8,128)(2,1)}, bf16[2,512,2,64]{1,3,2,0:T(8,128)(2,1)}, bf16[2,512,2,6...) while((s32[]{:T(128)}, bf16[1024,2,64]{0,2,1:T(8,128)(2,1)}, ...), condition=%wide.region_23.24_spmd.clone, body=%wide.region_17.23_spmd.clone.sunk | while | flops 712179712 | bytes 56854912 | solution.py:91
  178.5 1.4 constant_dynamic-slice_fusion.7
  180.1 0.9 dynamic-slice_bitcast_fusion.2
  181.0 1.0 broadcast_compare_fusion.5
  182.1 2.1 fusion.187
  184.2 1.2 fusion.188
  185.4 1.5 fusion.191
  186.9 2.8 convert_reduce_fusion.5
  189.7 1.9 fusion.189
  191.6 1.5 fusion.190
  193.2 1.5 fusion.192
  195.4 1.3 constant_dynamic-slice_fusion.7
  196.8 0.9 dynamic-slice_bitcast_fusion.2
  197.8 1.0 broadcast_compare_fusion.5
  198.8 2.1 fusion.187
  200.9 1.2 fusion.188
  202.1 1.5 fusion.191
  203.6 2.8 convert_reduce_fusion.5
  206.4 1.9 fusion.189
  208.4 1.5 fusion.190
  209.9 1.5 fusion.192
  212.2 1.2 copy.129
  213.4 0.9 reshape.375
  214.3 1.7 convolution_bitcast_fusion.1
  216.0 1.7 convolution_bitcast_fusion.2
  218.5 1.3 copy.133
  219.7 10.3 %all-to-all-start.1 = ((f32[64,16,3,128]{3,1,2,0:T(8,128)}), f32[64,16,3,128]{3,1,2,0:T(8,128)S(1)}, u32[]{:S(2)}, u32[]{:S(2)}) async-start(f32[64,16,3,128]{3,1,2,0:T(8,128)} %copy.133), calls=%async_computation.1 | async-start | bytes 3145728 | tf_op jit(solution)/shard_map/all_to_all | solution.py:45
  230.0 1.4 reduce_sum.227
  231.5 1.1 reduce_sum.228
  232.6 1.2 broadcast_divide_fusion.1
  233.8 35.2 %all-to-all-done.1 = f32[64,16,3,128]{3,1,2,0:T(8,128)S(1)} async-done(((f32[64,16,3,128]{3,1,2,0:T(8,128)}), f32[64,16,3,128]{3,1,2,0:T(8,128)S(1)}, u32[]{:S(2)}, u32[]{:S(2)}) %all-to-all-start.1) | async-done | bytes 1572896 | tf_op jit(solution)/shard_map/all_to_all | solution.py:45
  269.1 1.2 broadcast_divide_fusion
  (141 shorter events, 11.2 us)
Async XLA Ops:
  7.2 57.2 %copy-start = (bf16[200,1024]{1,0:T(8,128)(2,1)S(1)}, bf16[200,1024]{1,0:T(8,128)(2,1)}, u32[]{:S(2)}) copy-start(bf16[200,1024]{1,0:T(8,128)(2,1)} %param.24) | copy-start | bytes 1228804
  7.2 18.5 %copy-start.24 = (s32[1,4]{1,0:T(1,128)S(1)}, s32[1,4]{1,0:T(1,128)}, u32[]{:S(2)}) copy-start(s32[1,4]{1,0:T(1,128)} %param.20) | copy-start | bytes 52
  7.2 18.6 %copy-start.21 = (bf16[1024]{0:T(1024)(128)(2,1)S(1)}, bf16[1024]{0:T(1024)(128)(2,1)}, u32[]{:S(2)}) copy-start(bf16[1024]{0:T(1024)(128)(2,1)} %param.25) | copy-start | bytes 6148
  7.2 19.1 %copy-start.23 = (s32[1,4]{1,0:T(1,128)S(1)}, s32[1,4]{1,0:T(1,128)}, u32[]{:S(2)}) copy-start(s32[1,4]{1,0:T(1,128)} %param.23) | copy-start | bytes 52
  7.2 19.1 %copy-start.25 = (s32[1,4]{1,0:T(1,128)S(1)}, s32[1,4]{1,0:T(1,128)}, u32[]{:S(2)}) copy-start(s32[1,4]{1,0:T(1,128)} %param.22) | copy-start | bytes 52
  7.2 19.1 %copy-start.26 = (s32[1,4]{1,0:T(1,128)S(1)}, s32[1,4]{1,0:T(1,128)}, u32[]{:S(2)}) copy-start(s32[1,4]{1,0:T(1,128)} %param.21) | copy-start | bytes 52
  12.4 36.5 %all-to-all-start = ((bf16[64,2,3200]{2,1,0:T(2,128)(2,1)}), bf16[64,2,3200]{2,1,0:T(2,128)(2,1)S(1)}, u32[]{:S(2)}, u32[]{:S(2)}) async-start(bf16[64,2,3200]{2,1,0:T(2,128)(2,1)} %copy.118), calls=%async_computation | async-start | bytes 1638400 | tf_op jit(solution)/shard_map/all_to_all | solution.py:13
  25.6 125.4 %all-reduce.2.cloned.1.call-start = ((), (), s32[]{:S(2)}) async-start(), calls=%async_computation.4 | async-start | bytes 4194304 | tf_op jit(solution)/shard_map/psum | solution.py:175
  65.2 2.2 copy-start.1
  65.2 1.7 copy-start.27
  66.9 1.4 copy-start.2
  70.4 16.2 %copy-start.4 = (bf16[128,1024]{1,0:T(8,128)(2,1)S(1)}, bf16[128,1024]{1,0:T(8,128)(2,1)}, u32[]{:S(2)}) copy-start(bf16[128,1024]{1,0:T(8,128)(2,1)} %param.27) | copy-start | bytes 786436
  86.5 14.8 %copy-start.8 = (s32[1,1024]{1,0:T(1,128)}, s32[1,1024]{1,0:T(1,128)S(1)}, u32[]{:S(2)}) copy-start(s32[1,1024]{1,0:T(1,128)S(1)} %get-tuple-element.700) | copy-start | bytes 12292
  86.5 14.8 %copy-start.11 = (bf16[2,512,128]{2,1,0:T(8,128)(2,1)}, bf16[2,512,128]{2,1,0:T(8,128)(2,1)S(1)}, u32[]{:S(2)}) copy-start(bf16[2,512,128]{2,1,0:T(8,128)(2,1)S(1)} %get-tuple-element.271) | copy-start | bytes 786436
  86.5 14.8 %copy-start.18 = (s32[2,512]{1,0:T(2,128)}, s32[2,512]{1,0:T(2,128)S(1)}, u32[]{:S(2)}) copy-start(s32[2,512]{1,0:T(2,128)S(1)} %get-tuple-element.701) | copy-start | bytes 12292
  86.6 14.8 %copy-start.28 = (bf16[1024,2,64]{0,2,1:T(8,128)(2,1)}, bf16[1024,2,64]{0,2,1:T(8,128)(2,1)S(1)}, u32[]{:S(2)}) copy-start(bf16[1024,2,64]{0,2,1:T(8,128)(2,1)S(1)} %get-tuple-element.702) | copy-start | bytes 786436
  86.6 14.8 %copy-start.30 = (bf16[1024,2,64]{0,2,1:T(8,128)(2,1)}, bf16[1024,2,64]{0,2,1:T(8,128)(2,1)S(1)}, u32[]{:S(2)}) copy-start(bf16[1024,2,64]{0,2,1:T(8,128)(2,1)S(1)} %get-tuple-element.703) | copy-start | bytes 786436
  86.6 12.2 %copy-start.22 = (bf16[1024]{0:T(1024)(128)(2,1)S(1)}, bf16[1024]{0:T(1024)(128)(2,1)}, u32[]{:S(2)}) copy-start(bf16[1024]{0:T(1024)(128)(2,1)} %param.28) | copy-start | bytes 6148
  90.0 76.9 %all-to-all-start.2 = ((f32[64,1,1]{2,1,0:T(1,128)}), f32[64,1,1]{2,1,0:T(1,128)}, u32[]{:S(2)}, u32[]{:S(2)}) async-start(f32[64,1,1]{2,1,0:T(1,128)} %broadcast_in_dim.203), calls=%async_computation.2 | async-start | bytes 65536 | tf_op jit(solution)/shard_map/all_to_all | solution.py:28
  101.3 53.8 %copy-start.9 = (f32[1024,100]{0,1:T(8,128)S(1)}, f32[1024,100]{0,1:T(8,128)}, u32[]{:S(2)}) copy-start(f32[1024,100]{0,1:T(8,128)} %copy.126) | copy-start | bytes 1228804
  101.3 53.8 %copy-start.10 = (f32[1024,100]{0,1:T(8,128)S(1)}, f32[1024,100]{0,1:T(8,128)}, u32[]{:S(2)}) copy-start(f32[1024,100]{0,1:T(8,128)} %copy.125) | copy-start | bytes 1228804
  101.3 53.8 %copy-start.19 = (f32[1024]{0:T(1024)S(1)}, f32[1024]{0:T(1024)}, u32[]{:S(2)}) copy-start(f32[1024]{0:T(1024)} %convert_element_type.206) | copy-start | bytes 12292
  101.4 53.8 %copy-start.20 = (f32[1024]{0:T(1024)S(1)}, f32[1024]{0:T(1024)}, u32[]{:S(2)}) copy-start(f32[1024]{0:T(1024)} %get-tuple-element.492) | copy-start | bytes 12292
  159.5 3.2 %copy-start.12 = (bf16[2,512,128]{2,1,0:T(8,128)(2,1)S(1)}, bf16[2,512,128]{2,1,0:T(8,128)(2,1)}, u32[]{:S(2)}) copy-start(bf16[2,512,128]{2,1,0:T(8,128)(2,1)} %copy-done.11) | copy-start | bytes 786436
  159.5 5.5 %copy-start.5 = (bf16[128,1024]{1,0:T(8,128)(2,1)S(1)}, bf16[128,1024]{1,0:T(8,128)(2,1)}, u32[]{:S(2)}) copy-start(bf16[128,1024]{1,0:T(8,128)(2,1)} %param.27) | copy-start | bytes 786436
  166.9 52.8 %all-to-all-start.3 = ((f32[64,128,16]{1,2,0:T(8,128)}), f32[64,128,16]{1,2,0:T(8,128)}, u32[]{:S(2)}, u32[]{:S(2)}) async-start(f32[64,128,16]{1,2,0:T(8,128)} %copy.136), calls=%async_computation.3 | async-start | bytes 1048576 | tf_op jit(solution)/shard_map/all_to_all | solution.py:45
  178.5 35.7 %copy-start.3 = (bf16[1024,1024]{0,1:T(8,128)(2,1)S(1)}, bf16[1024,1024]{0,1:T(8,128)(2,1)}, u32[]{:S(2)}) copy-start(bf16[1024,1024]{0,1:T(8,128)(2,1)} %copy-done.2) | copy-start | bytes 6291460
  182.1 3.3 %copy-start.13 = (bf16[1024,2,64]{0,2,1:T(8,128)(2,1)S(1)}, bf16[1024,2,64]{0,2,1:T(8,128)(2,1)}, u32[]{:S(2)}) copy-start(bf16[1024,2,64]{0,2,1:T(8,128)(2,1)} %get-tuple-element.672) | copy-start | bytes 786436 | tf_op jit(solution)/shard_map/transpose(jvp())/while
  185.4 1.5 copy-start.29
  186.8 2.8 %copy-start.14 = (bf16[1024,2,64]{0,2,1:T(8,128)(2,1)}, bf16[1024,2,64]{0,2,1:T(8,128)(2,1)S(1)}, u32[]{:S(2)}) copy-start(bf16[1024,2,64]{0,2,1:T(8,128)(2,1)S(1)} %fusion.191) | copy-start | bytes 786436 | tf_op jit(solution)/shard_map/transpose(jvp())/while
  189.7 1.9 copy-start.16
  191.6 1.6 copy-start.6
  191.6 1.6 copy-start.31
  193.2 1.5 copy-start.17
  194.7 0.7 copy-start.7
  198.8 3.3 %copy-start.13 = (bf16[1024,2,64]{0,2,1:T(8,128)(2,1)S(1)}, bf16[1024,2,64]{0,2,1:T(8,128)(2,1)}, u32[]{:S(2)}) copy-start(bf16[1024,2,64]{0,2,1:T(8,128)(2,1)} %get-tuple-element.672) | copy-start | bytes 786436 | tf_op jit(solution)/shard_map/transpose(jvp())/while
  202.1 1.5 copy-start.29
  203.6 2.8 %copy-start.14 = (bf16[1024,2,64]{0,2,1:T(8,128)(2,1)}, bf16[1024,2,64]{0,2,1:T(8,128)(2,1)S(1)}, u32[]{:S(2)}) copy-start(bf16[1024,2,64]{0,2,1:T(8,128)(2,1)S(1)} %fusion.191) | copy-start | bytes 786436 | tf_op jit(solution)/shard_map/transpose(jvp())/while
  206.4 1.9 copy-start.16
  208.3 1.6 copy-start.6
  208.3 1.6 copy-start.31
  209.9 1.5 copy-start.17
  211.4 0.7 copy-start.7
  214.2 3.4 %copy-start.15 = (bf16[1024,2,64]{0,2,1:T(8,128)(2,1)S(1)}, bf16[1024,2,64]{0,2,1:T(8,128)(2,1)}, u32[]{:S(2)}) copy-start(bf16[1024,2,64]{0,2,1:T(8,128)(2,1)} %get-tuple-element.274) | copy-start | bytes 786436
  219.7 49.3 %all-to-all-start.1 = ((f32[64,16,3,128]{3,1,2,0:T(8,128)}), f32[64,16,3,128]{3,1,2,0:T(8,128)S(1)}, u32[]{:S(2)}, u32[]{:S(2)}) async-start(f32[64,16,3,128]{3,1,2,0:T(8,128)} %copy.133), calls=%async_computation.1 | async-start | bytes 3145728 | tf_op jit(solution)/shard_map/all_to_all | solution.py:45
Sparse Core Ops, SparseCore 0:
  88.8 62.0 all-reduce.1
where the time goes:
time: 278 us; the launch traced here: 277 us
  waiting for transfers between devices  106 us (38%)
  matrix products  52.6 us (19%)
  starting transfers between devices  43.1 us (16%)
  other arithmetic  25.4 us (9%)
  local copies, waits for them, and re-layouts  23.7 us (9%)
  between operations  14.6 us (5%)
  blocking collectives  11.4 us (4%)
    psum x1, waiting for transfers between devices, shards(): mixed = lax.psum(partial_mix.astype(jnp.bfloat16), 'mp').astype(jnp.float32)  49.6 us
    all_to_all x2, waiting for transfers between devices, sent_and_summed(): tiles = lax.all_to_all(split_up(shard, dim, length), axis, 0, 0, tiled=True)  35.2 us
    all_to_all x2, starting transfers between devices, sent_and_summed(): tiles = lax.all_to_all(split_up(shard, dim, length), axis, 0, 0, tiled=True)  21.2 us
    all_to_all x1, waiting for transfers between devices, sent_together(): lax.all_to_all(both, axis, split_axis=split_dim, concat_axis=concat_dim,...  21.2 us
    dot_general x6, matrix products, one_block(): jnp.einsum('hqk,khd->qhd', probs, valued, preferred_element_type=jnp.floa...  14.5 us
    all_to_all x1, starting transfers between devices, sent_together(): lax.all_to_all(both, axis, split_axis=split_dim, concat_axis=concat_dim,...  13.2 us
    all_gather x1, blocking collectives, sent_together_2(): lax.all_gather(both, axis, axis=dim, tiled=True)  11.4 us
    dot_general x6, matrix products, one_block(): jnp.einsum('qhd,khd->hqk', query_block, keyed, preferred_element_type=jnp...  10.2 us
  transfers between devices with their start and end apart: 5, of which 3 were waited for; matrix products, arithmetic and copies ran while one was open for 24% of the time, Pallas kernels for 0%

commit v1 on v0

--- a/solution.py
+++ b/solution.py
@@ -172,7 +172,9 @@
     heads_out, pullback = jax.vjp(lambda a, b, c: attend(a, b, c, segment), query, keys, values)
     attended = heads_out.astype(jnp.bfloat16)
     partial_mix = jnp.dot(attended, out_proj, preferred_element_type=jnp.float32)
-    mixed = lax.psum(partial_mix.astype(jnp.bfloat16), "mp").astype(jnp.float32)
+    mixed = jnp.sum(lax.all_gather(partial_mix.astype(jnp.bfloat16), "mp"), axis=0).astype(
+        jnp.float32
+    )
     hidden1 = (hidden0 + mixed).astype(jnp.bfloat16)
     wide1 = lax.optimization_barrier(hidden1).astype(jnp.float32)
     rscale = lax.rsqrt(jnp.mean(wide1 * wide1, axis=1, keepdims=True) + 1e-06)

time: 278 us -> 320 us (1.15); the launches traced: 277 us -> 316 us
  waiting for transfers between devices: 106 us -> 130 us
  matrix products: 52.6 us -> 64.7 us
    all_gather x0 -> x1, waiting for transfers between devices: none -> 72.1 us  [shards(): lax.all_gather(partial_mix.astype(jnp.bfloat16), 'mp')]
    psum x1 -> x0, waiting for transfers between devices: 49.6 us -> none  [shards(): mixed = lax.psum(partial_mix.astype(jnp.bfloat16), 'mp').astype(jnp.float32)]
    reduce_sum x0 -> x1, other arithmetic: none -> 6.5 us  [shards(): jnp.sum(lax.all_gather(partial_mix.astype(jnp.bfloat16), 'mp'), axis=0)]
    dot_general x6, matrix products: 14.5 us -> 20.5 us  [one_block(): jnp.einsum('hqk,khd->qhd', probs, valued, preferred_element_type=jnp.floa...]
    dot_general x6, matrix products: 10.2 us -> 15.9 us  [one_block(): jnp.einsum('qhd,khd->hqk', query_block, keyed, preferred_element_type=jnp...]
where the time goes in v1:
time: 320 us; the launch traced here: 316 us
  waiting for transfers between devices  130 us (41%)
  matrix products  64.7 us (20%)
  starting transfers between devices  43.1 us (13%)
  other arithmetic  28.5 us (9%)
  local copies, waits for them, and re-layouts  22.5 us (7%)
  between operations  14.7 us (5%)
  blocking collectives  11.7 us (4%)
    all_gather x1, waiting for transfers between devices, shards(): lax.all_gather(partial_mix.astype(jnp.bfloat16), 'mp')  72.1 us
    all_to_all x2, waiting for transfers between devices, sent_and_summed(): tiles = lax.all_to_all(split_up(shard, dim, length), axis, 0, 0, tiled=True)  36 us
    all_to_all x1, waiting for transfers between devices, sent_together(): lax.all_to_all(both, axis, split_axis=split_dim, concat_axis=concat_dim,...  21.9 us
    all_to_all x2, starting transfers between devices, sent_and_summed(): tiles = lax.all_to_all(split_up(shard, dim, length), axis, 0, 0, tiled=True)  21.2 us
    dot_general x6, matrix products, one_block(): jnp.einsum('hqk,khd->qhd', probs, valued, preferred_element_type=jnp.floa...  20.5 us
    dot_general x6, matrix products, one_block(): jnp.einsum('qhd,khd->hqk', query_block, keyed, preferred_element_type=jnp...  15.9 us
    all_to_all x1, starting transfers between devices, sent_together(): lax.all_to_all(both, axis, split_axis=split_dim, concat_axis=concat_dim,...  13.2 us
    all_gather x1, blocking collectives, sent_together_2(): lax.all_gather(both, axis, axis=dim, tiled=True)  11.7 us
  transfers between devices with their start and end apart: 5, of which 3 were waited for; matrix products, arithmetic and copies ran while one was open for 24% of the time, Pallas kernels for 0%

profile of v1, /device:TPU:1, one launch (start us, length us, event | category | flops | bytes accessed | tf_op | source)
XLA Modules:
  0.0 315.5 jit_solution(10893198668680579485)
XLA Ops:
  7.3 0.8 eq.126
  8.4 1.1 fusion.61
  9.5 1.1 fusion.62
  10.7 1.7 copy.116
  12.4 13.2 %all-to-all-start = ((bf16[64,2,3200]{2,1,0:T(2,128)(2,1)}), bf16[64,2,3200]{2,1,0:T(2,128)(2,1)S(1)}, u32[]{:S(2)}, u32[]{:S(2)}) async-start(bf16[64,2,3200]{2,1,0:T(2,128)(2,1)} %copy.116), calls=%async_computation | async-start | bytes 1638400 | tf_op jit(solution)/shard_map/all_to_all | solution.py:13
  27.0 21.9 %all-to-all-done = bf16[64,2,3200]{2,1,0:T(2,128)(2,1)S(1)} async-done(((bf16[64,2,3200]{2,1,0:T(2,128)(2,1)}), bf16[64,2,3200]{2,1,0:T(2,128)(2,1)S(1)}, u32[]{:S(2)}, u32[]{:S(2)}) %all-to-all-start) | async-done | bytes 819232 | tf_op jit(solution)/shard_map/all_to_all | solution.py:13
  48.9 1.1 fusion.127
  50.5 11.7 %all_gather.9 = bf16[16,12800]{1,0:T(8,128)(2,1)S(1)} all-gather(bf16[16,3200]{1,0:T(8,128)(2,1)S(1)} %pad_maximum_fusion.2), channel_id=1, replica_groups=mesh['dp'=64,'mp'=4] {'mp'}, dimensions={1}, use_global_device_ids=true | all-gather | bytes 512000 | tf_op jit(solution)/shard_map/all_gather | solution.py:19
  62.2 0.9 reshape.364
  63.2 0.9 reshape.365
  64.6 0.9 multiply_reduce_fusion
  65.9 1.3 copy-done.16
  67.2 0.8 convolution_convert_fusion.9
  68.0 1.2 convolution_convert_fusion.8
  69.2 1.2 convolution_convert_fusion.7
  71.0 16.2 %while.30 = (s32[]{:T(128)}, bf16[2,512,128]{2,1,0:T(8,128)(2,1)S(1)}, s32[2,512]{1,0:T(2,128)S(1)}, s32[1,1024]{1,0:T(1,128)S(1)}, bf16[2,512,2,64]{1,3,2,0:T(8...) while((s32[]{:T(128)}, bf16[2,512,128]{2,1,0:T(8,128)(2,1)S(1)}, ...), condition=%wide.region_13.14_spmd, body=%wide.region_10.13_spmd.sunk | while | flops 275252224 | bytes 11815037 | solution.py:91
  71.4 4.5 %fusion.178 = (f32[2,512]{1,0:T(2,128)S(1)}, f32[2,512,1024]{2,1,0:T(8,128)}) fusion(pred[512,1024]{1,0:T(8,128)(4,1)S(1)} %broadcast_compare_fusion.4, bf16[1024,2,64]{0,2,1:T(8,128)(2,1)} %get-tuple-element.655, bf16[2,512,2,64]{1,3,2,0:T(8,128)(2,1)S(1)} %get-tuple-element.654, s32[]{:T(128)} %get-tuple-element.642), kind=kOutput, calls=%fused_computation.183.clone.1 | convolution fusion | flops 138413056 | bytes 5115908 | tf_op jit(solution)/shard_map/jvp()/while/body/eval_jaxpr/sub | solution.py:85
  75.9 3.0 fusion.179
  79.5 4.5 %fusion.178 = (f32[2,512]{1,0:T(2,128)S(1)}, f32[2,512,1024]{2,1,0:T(8,128)}) fusion(pred[512,1024]{1,0:T(8,128)(4,1)S(1)} %broadcast_compare_fusion.4, bf16[1024,2,64]{0,2,1:T(8,128)(2,1)} %get-tuple-element.655, bf16[2,512,2,64]{1,3,2,0:T(8,128)(2,1)S(1)} %get-tuple-element.654, s32[]{:T(128)} %get-tuple-element.642), kind=kOutput, calls=%fused_computation.183.clone.1 | convolution fusion | flops 138413056 | bytes 5115908 | tf_op jit(solution)/shard_map/jvp()/while/body/eval_jaxpr/sub | solution.py:85
  84.0 3.0 fusion.179
  87.2 2.0 convolution_convert_fusion.5
  89.3 1.3 broadcast_in_dim.203
  90.6 8.8 %all-to-all-start.2 = ((f32[64,1,1]{2,1,0:T(1,128)}), f32[64,1,1]{2,1,0:T(1,128)S(1)}, u32[]{:S(2)}, u32[]{:S(2)}) async-start(f32[64,1,1]{2,1,0:T(1,128)} %broadcast_in_dim.203), calls=%async_computation.2 | async-start | bytes 65536 | tf_op jit(solution)/shard_map/all_to_all | solution.py:28
  99.4 1.0 copy.123
  100.3 1.0 copy.124
  101.3 72.1 %all-gather.3.cloned.1.call-done = bf16[4096,1024]{1,0:T(8,128)(2,1)} async-done(((bf16[1024,1024]{1,0:T(8,128)(2,1)}), bf16[4096,1024]{1,0:T(8,128)(2,1)}) %all-gather.3.cloned.1.call-update) | async-done | bytes 8388624 | tf_op jit(solution)/shard_map/all_gather | solution.py:175
  173.4 6.5 %reduce_sum.235 = bf16[1024,1024]{1,0:T(8,128)(2,1)S(1)} reduce(bf16[4,1024,1024]{2,1,0:T(8,128)(2,1)} %bitcast.172, bf16[]{:T(256)} %constant.190.clone.1), dimensions={0}, to_apply=%region_14.15 | reduce | flops 3145728 | bytes 10485762 | tf_op jit(solution)/shard_map/reduce_sum | solution.py:175
  179.9 2.6 copy.122
  182.5 3.7 %add_convert_fusion = bf16[1024,1024]{0,1:T(8,128)(2,1)S(1)} fusion(f32[1024,1024]{0,1:T(8,128)} %copy-done.5, bf16[1024,1024]{0,1:T(8,128)(2,1)} %copy.122), kind=kLoop, calls=%fused_computation.86 | loop fusion | flops 3145728 | bytes 8388608 | tf_op jit(solution)/shard_map/convert_element_type | solution.py:178
  186.6 4.5 %fusion.64 = (f32[1024]{0:T(1024)S(1)}, f32[1024,1024]{0,1:T(8,128)}) fusion(bf16[1024,1024]{0,1:T(8,128)(2,1)S(1)} %add_convert_fusion, f32[1024]{0:T(1024)S(1)} %convert_element_type.208, f32[1024]{0:T(1024)S(1)} %add_rsqrt_fusion, bf16[1024,100]{0,1:T(8,128)(2,1)S(1)} %copy-done.17, f32[1024,100]{0,1:T(8,128)} %copy.123, f32[1024,100]{0,1:T(8,128)} %copy.124, ...), kind=kOutput, calls=%fused_computation.81 | convolution fusion | flops 429276160 | bytes 7331840 | tf_op jit(solution)/shard_map/dot_general | solution.py:187
  191.1 3.1 fusion.67
  194.2 2.3 fusion.75
  196.6 0.8 convolution_convert_fusion.6
  197.4 1.1 copy.134
  198.5 10.9 %all-to-all-start.3 = ((f32[64,128,16]{1,2,0:T(8,128)}), f32[64,128,16]{1,2,0:T(8,128)}, u32[]{:S(2)}, u32[]{:S(2)}) async-start(f32[64,128,16]{1,2,0:T(8,128)} %copy.134), calls=%async_computation.3 | async-start | bytes 1048576 | tf_op jit(solution)/shard_map/all_to_all | solution.py:45
  209.4 0.7 broadcast_in_dim.200
  210.1 41.8 %while.31 = (s32[]{:T(128)}, bf16[1024,2,64]{0,2,1:T(8,128)(2,1)}, bf16[1024,2,64]{0,2,1:T(8,128)(2,1)}, bf16[2,512,2,64]{1,3,2,0:T(8,128)(2,1)}, bf16[2,512,2,6...) while((s32[]{:T(128)}, bf16[1024,2,64]{0,2,1:T(8,128)(2,1)}, ...), condition=%wide.region_23.24_spmd.clone, body=%wide.region_17.23_spmd.clone.sunk | while | flops 712179712 | bytes 108235080 | solution.py:91
  210.7 2.1 fusion.187
  212.8 1.2 fusion.188
  214.0 2.8 convert_reduce_fusion.5
  216.8 1.9 fusion.189
  218.7 1.9 copy-done.3
  220.7 3.1 fusion.192
  223.8 4.5 %fusion.191 = bf16[1024,2,64]{0,2,1:T(8,128)(2,1)} fusion(bf16[2,64,512]{2,1,0:T(8,128)(2,1)S(1)} %bitcast.175, f32[2,512]{1,0:T(2,128)S(1)} %fusion.188, f32[2,512,1024]{2,1,0:T(8,128)} %copy-done.2, f32[2,512]{1,0:T(2,128)S(1)} %get-tuple-element.624, pred[512,1024]{1,0:T(8,128)(4,1)S(1)} %broadcast_compare_fusion.5, ...), kind=kOutput, calls=%fused_computation.52.clone.1 | convolution fusion | flops 139722752 | bytes 5382145 | tf_op jit(solution)/shard_map/transpose(jvp())/while/body/eval_jaxpr/checkpoint/hqk,khd->qhd/dot_general | solution.py:87
  228.3 2.3 fusion.190
  231.1 2.1 fusion.187
  233.2 1.2 fusion.188
  234.4 2.8 convert_reduce_fusion.5
  237.2 1.9 fusion.189
  239.1 1.9 copy-done.3
  241.0 3.1 fusion.192
  244.2 4.5 %fusion.191 = bf16[1024,2,64]{0,2,1:T(8,128)(2,1)} fusion(bf16[2,64,512]{2,1,0:T(8,128)(2,1)S(1)} %bitcast.175, f32[2,512]{1,0:T(2,128)S(1)} %fusion.188, f32[2,512,1024]{2,1,0:T(8,128)} %copy-done.2, f32[2,512]{1,0:T(2,128)S(1)} %get-tuple-element.624, pred[512,1024]{1,0:T(8,128)(4,1)S(1)} %broadcast_compare_fusion.5, ...), kind=kOutput, calls=%fused_computation.52.clone.1 | convolution fusion | flops 139722752 | bytes 5382145 | tf_op jit(solution)/shard_map/transpose(jvp())/while/body/eval_jaxpr/checkpoint/hqk,khd->qhd/dot_general | solution.py:87
  248.7 3.2 %fusion.190 = bf16[1024,2,64]{0,2,1:T(8,128)(2,1)} fusion(bf16[512,2,64]{0,2,1:T(8,128)(2,1)S(1)} %dynamic-slice_bitcast_fusion.2, f32[2,512,1024]{2,1,0:T(8,128)S(1)} %copy-done.4, pred[2,512,1024]{2,1,0:T(32,128)(4,1)S(1)} %copy-done.21, f32[2,512]{1,0:T(2,128)S(1)} %negate_divide_fusion.2, pred[512,1024]{1,0:T(8,128)(4,1)S(1)} %broadcast_compare_fusion.5, ...), kind=kOutput, calls=%fused_computation.53.clone.1 | convolution fusion | flops 138805248 | bytes 6426625 | tf_op jit(solution)/shard_map/transpose(jvp())/while/body/eval_jaxpr/checkpoint/qhd,khd->hqk/dot_general | solution.py:80
  251.9 1.3 copy.127
  253.3 0.7 convolution_bitcast_fusion.2
  254.0 1.7 convolution_bitcast_fusion.1
  255.7 0.7 convolution_bitcast_fusion
  256.5 1.3 copy.131
  257.8 10.3 %all-to-all-start.1 = ((f32[64,16,3,128]{3,1,2,0:T(8,128)}), f32[64,16,3,128]{3,1,2,0:T(8,128)S(1)}, u32[]{:S(2)}, u32[]{:S(2)}) async-start(f32[64,16,3,128]{3,1,2,0:T(8,128)} %copy.131), calls=%async_computation.1 | async-start | bytes 3145728 | tf_op jit(solution)/shard_map/all_to_all | solution.py:45
  268.1 0.7 reduce_sum.240
  268.8 1.1 reduce_sum.241
  269.9 1.2 broadcast_divide_fusion.1
  271.1 36.0 %all-to-all-done.1 = f32[64,16,3,128]{3,1,2,0:T(8,128)S(1)} async-done(((f32[64,16,3,128]{3,1,2,0:T(8,128)}), f32[64,16,3,128]{3,1,2,0:T(8,128)S(1)}, u32[]{:S(2)}, u32[]{:S(2)}) %all-to-all-start.1) | async-done | bytes 1572896 | tf_op jit(solution)/shard_map/all_to_all | solution.py:45
  307.2 1.2 broadcast_divide_fusion
  (121 shorter events, 7.0 us)
Async XLA Ops:
  7.2 57.5 %copy-start = (bf16[200,1024]{1,0:T(8,128)(2,1)S(1)}, bf16[200,1024]{1,0:T(8,128)(2,1)}, u32[]{:S(2)}) copy-start(bf16[200,1024]{1,0:T(8,128)(2,1)} %param.24) | copy-start | bytes 1228804
  7.2 18.5 %copy-start.13 = (s32[1,4]{1,0:T(1,128)S(1)}, s32[1,4]{1,0:T(1,128)}, u32[]{:S(2)}) copy-start(s32[1,4]{1,0:T(1,128)} %param.20) | copy-start | bytes 52
  7.2 18.6 %copy-start.10 = (bf16[1024]{0:T(1024)(128)(2,1)S(1)}, bf16[1024]{0:T(1024)(128)(2,1)}, u32[]{:S(2)}) copy-start(bf16[1024]{0:T(1024)(128)(2,1)} %param.25) | copy-start | bytes 6148
  7.2 19.1 %copy-start.15 = (s32[1,4]{1,0:T(1,128)S(1)}, s32[1,4]{1,0:T(1,128)}, u32[]{:S(2)}) copy-start(s32[1,4]{1,0:T(1,128)} %param.21) | copy-start | bytes 52
  7.2 19.1 %copy-start.14 = (s32[1,4]{1,0:T(1,128)S(1)}, s32[1,4]{1,0:T(1,128)}, u32[]{:S(2)}) copy-start(s32[1,4]{1,0:T(1,128)} %param.22) | copy-start | bytes 52
  7.2 19.1 %copy-start.12 = (s32[1,4]{1,0:T(1,128)S(1)}, s32[1,4]{1,0:T(1,128)}, u32[]{:S(2)}) copy-start(s32[1,4]{1,0:T(1,128)} %param.23) | copy-start | bytes 52
  12.4 36.5 %all-to-all-start = ((bf16[64,2,3200]{2,1,0:T(2,128)(2,1)}), bf16[64,2,3200]{2,1,0:T(2,128)(2,1)S(1)}, u32[]{:S(2)}, u32[]{:S(2)}) async-start(bf16[64,2,3200]{2,1,0:T(2,128)(2,1)} %copy.116), calls=%async_computation | async-start | bytes 1638400 | tf_op jit(solution)/shard_map/all_to_all | solution.py:13
  25.6 147.8 %all-gather.3.cloned.1.call-start = ((), (), s32[]{:S(2)}) async-start(), calls=%async_computation.4 | async-start | bytes 10485760 | tf_op jit(solution)/shard_map/all_gather | solution.py:175
  65.5 2.5 copy-start.5
  65.5 1.7 copy-start.16
  67.2 2.0 copy-start.6
  71.0 16.2 %copy-start.8 = (bf16[128,1024]{1,0:T(8,128)(2,1)S(1)}, bf16[128,1024]{1,0:T(8,128)(2,1)}, u32[]{:S(2)}) copy-start(bf16[128,1024]{1,0:T(8,128)(2,1)} %param.27) | copy-start | bytes 786436
  71.1 4.9 %copy-start.18 = (bf16[1024,2,64]{0,2,1:T(8,128)(2,1)S(1)}, bf16[1024,2,64]{0,2,1:T(8,128)(2,1)}, u32[]{:S(2)}) copy-start(bf16[1024,2,64]{0,2,1:T(8,128)(2,1)} %get-tuple-element.656) | copy-start | bytes 786436 | tf_op jit(solution)/shard_map/jvp()/while
  79.2 4.9 %copy-start.18 = (bf16[1024,2,64]{0,2,1:T(8,128)(2,1)S(1)}, bf16[1024,2,64]{0,2,1:T(8,128)(2,1)}, u32[]{:S(2)}) copy-start(bf16[1024,2,64]{0,2,1:T(8,128)(2,1)} %get-tuple-element.656) | copy-start | bytes 786436 | tf_op jit(solution)/shard_map/jvp()/while
  87.2 12.1 %copy-start.11 = (bf16[1024]{0:T(1024)(128)(2,1)S(1)}, bf16[1024]{0:T(1024)(128)(2,1)}, u32[]{:S(2)}) copy-start(bf16[1024]{0:T(1024)(128)(2,1)} %param.28) | copy-start | bytes 6148
  90.6 107.9 %all-to-all-start.2 = ((f32[64,1,1]{2,1,0:T(1,128)}), f32[64,1,1]{2,1,0:T(1,128)S(1)}, u32[]{:S(2)}, u32[]{:S(2)}) async-start(f32[64,1,1]{2,1,0:T(1,128)} %broadcast_in_dim.203), calls=%async_computation.2 | async-start | bytes 65536 | tf_op jit(solution)/shard_map/all_to_all | solution.py:28
  182.5 4.2 %copy-start.17 = (bf16[1024,100]{0,1:T(8,128)(2,1)S(1)}, bf16[1024,100]{0,1:T(8,128)(2,1)}, u32[]{:S(2)}) copy-start(bf16[1024,100]{0,1:T(8,128)(2,1)} %param.29) | copy-start | bytes 614404
  198.5 59.3 %all-to-all-start.3 = ((f32[64,128,16]{1,2,0:T(8,128)}), f32[64,128,16]{1,2,0:T(8,128)}, u32[]{:S(2)}, u32[]{:S(2)}) async-start(f32[64,128,16]{1,2,0:T(8,128)} %copy.134), calls=%async_computation.3 | async-start | bytes 1048576 | tf_op jit(solution)/shard_map/all_to_all | solution.py:45
  210.1 43.2 %copy-start.7 = (bf16[1024,1024]{0,1:T(8,128)(2,1)S(1)}, bf16[1024,1024]{0,1:T(8,128)(2,1)}, u32[]{:S(2)}) copy-start(bf16[1024,1024]{0,1:T(8,128)(2,1)} %copy-done.6) | copy-start | bytes 6291460
  210.6 3.3 %copy-start.19 = (bf16[1024,2,64]{0,2,1:T(8,128)(2,1)S(1)}, bf16[1024,2,64]{0,2,1:T(8,128)(2,1)}, u32[]{:S(2)}) copy-start(bf16[1024,2,64]{0,2,1:T(8,128)(2,1)} %get-tuple-element.627) | copy-start | bytes 786436 | tf_op jit(solution)/shard_map/transpose(jvp())/while
  212.8 4.0 %copy-start.2 = (f32[2,512,1024]{2,1,0:T(8,128)}, f32[2,512,1024]{2,1,0:T(8,128)S(1)}, u32[]{:S(2)}) copy-start(f32[2,512,1024]{2,1,0:T(8,128)S(1)} %get-tuple-element.625) | copy-start | bytes 12582916 | tf_op jit(solution)/shard_map/transpose(jvp())/while
  216.8 2.0 copy-start.20
  218.7 2.0 copy-start.3
  223.8 4.5 %copy-start.4 = (f32[2,512,1024]{2,1,0:T(8,128)S(1)}, f32[2,512,1024]{2,1,0:T(8,128)}, u32[]{:S(2)}) copy-start(f32[2,512,1024]{2,1,0:T(8,128)} %copy-done.3) | copy-start | bytes 12582916 | tf_op jit(solution)/shard_map/transpose(jvp())/while
  223.8 4.5 %copy-start.21 = (pred[2,512,1024]{2,1,0:T(32,128)(4,1)S(1)}, pred[2,512,1024]{2,1,0:T(32,128)(4,1)}, u32[]{:S(2)}) copy-start(pred[2,512,1024]{2,1,0:T(32,128)(4,1)} %copy-done.20) | copy-start | bytes 3145732 | tf_op jit(solution)/shard_map/transpose(jvp())/while
  231.1 3.3 %copy-start.19 = (bf16[1024,2,64]{0,2,1:T(8,128)(2,1)S(1)}, bf16[1024,2,64]{0,2,1:T(8,128)(2,1)}, u32[]{:S(2)}) copy-start(bf16[1024,2,64]{0,2,1:T(8,128)(2,1)} %get-tuple-element.627) | copy-start | bytes 786436 | tf_op jit(solution)/shard_map/transpose(jvp())/while
  233.2 4.0 %copy-start.2 = (f32[2,512,1024]{2,1,0:T(8,128)}, f32[2,512,1024]{2,1,0:T(8,128)S(1)}, u32[]{:S(2)}) copy-start(f32[2,512,1024]{2,1,0:T(8,128)S(1)} %get-tuple-element.625) | copy-start | bytes 12582916 | tf_op jit(solution)/shard_map/transpose(jvp())/while
  237.1 2.0 copy-start.20
  239.1 2.0 copy-start.3
  244.2 4.5 %copy-start.4 = (f32[2,512,1024]{2,1,0:T(8,128)S(1)}, f32[2,512,1024]{2,1,0:T(8,128)}, u32[]{:S(2)}) copy-start(f32[2,512,1024]{2,1,0:T(8,128)} %copy-done.3) | copy-start | bytes 12582916 | tf_op jit(solution)/shard_map/transpose(jvp())/while
  244.2 4.5 %copy-start.21 = (pred[2,512,1024]{2,1,0:T(32,128)(4,1)S(1)}, pred[2,512,1024]{2,1,0:T(32,128)(4,1)}, u32[]{:S(2)}) copy-start(pred[2,512,1024]{2,1,0:T(32,128)(4,1)} %copy-done.20) | copy-start | bytes 3145732 | tf_op jit(solution)/shard_map/transpose(jvp())/while
  251.9 3.8 %copy-start.9 = (bf16[1024,2,64]{0,2,1:T(8,128)(2,1)S(1)}, bf16[1024,2,64]{0,2,1:T(8,128)(2,1)}, u32[]{:S(2)}) copy-start(bf16[1024,2,64]{0,2,1:T(8,128)(2,1)} %get-tuple-element.274) | copy-start | bytes 786436
  256.4 52.0 %copy-start.1 = (bf16[200,1024]{1,0:T(8,128)(2,1)S(1)}, bf16[200,1024]{1,0:T(8,128)(2,1)}, u32[]{:S(2)}) copy-start(bf16[200,1024]{1,0:T(8,128)(2,1)} %param.24) | copy-start | bytes 1228804
  257.8 49.3 %all-to-all-start.1 = ((f32[64,16,3,128]{3,1,2,0:T(8,128)}), f32[64,16,3,128]{3,1,2,0:T(8,128)S(1)}, u32[]{:S(2)}, u32[]{:S(2)}) async-start(f32[64,16,3,128]{3,1,2,0:T(8,128)} %copy.131), calls=%async_computation.1 | async-start | bytes 3145728 | tf_op jit(solution)/shard_map/all_to_all | solution.py:45
Sparse Core Ops, SparseCore 0:
  89.4 83.9 all-gather.2
